TPU v7x, 32 devices: a whole 2x2x4 slice. The times are simulated.
32 devices in a mesh: dp: 8 (over y, x, core), tensor: 4 (over z).
Axes of the slice: x: 2, y: 2, z: 4, core: 2. Of those that a mesh axis runs over, the one named last changes fastest.
Arguments:
- tokens: bfloat16 [8192, 2048], P(('dp', 'tensor')), may hold values from -6 to 6
- positions: int32 [8192], P('dp'), may hold values from 0 to 1023, as said below
- norm_gain: float32 [2, 2, 2048], replicated, may hold values from 0.25 to 1.75
- norm_bias: float32 [2, 2, 2048], replicated, may hold values from -3 to 3
- w_qkv: bfloat16 [2, 2048, 3, 2048], P(None, 'dp', None, 'tensor'), may hold values from -0.125 to 0.125
- b_qkv: float32 [2, 3, 2048], replicated, may hold values from -3 to 3
- w_out: bfloat16 [2, 2048, 2048], P(None, 'tensor', 'dp'), may hold values from -0.5 to 0.5
- w_gate_up: bfloat16 [2, 2048, 2, 5632], P(None, 'dp', None, 'tensor'), may hold values from -0.125 to 0.125
- w_down: bfloat16 [2, 5632, 2048], P(None, 'tensor', 'dp'), may hold values from -0.078125 to 0.078125
- cotangent: bfloat16 [8192, 2048], P(('dp', 'tensor')), may hold values from -6 to 6
Outputs:
- activations: bfloat16 [8192, 2048], P(('dp', 'tensor'))
- input_grad: float32 [8192, 2048], P(('dp', 'tensor'))
- gain_grad: float32 [2, 2, 2048], replicated
- norm_bias_grad: float32 [2, 2, 2048], replicated
- qkv_grad: float32 [2, 2048, 3, 2048], P(None, 'dp', None, 'tensor')
- qkv_bias_grad: float32 [2, 3, 2048], replicated
- out_grad: float32 [2, 2048, 2048], P(None, 'tensor', 'dp')
- gate_up_grad: float32 [2, 2048, 2, 5632], P(None, 'dp', None, 'tensor')
- down_grad: float32 [2, 5632, 2048], P(None, 'tensor', 'dp')
Inputs may be any that keep to these rules, and one draw needn't show every extreme that they name: positions[i] counts the tokens before i in its document; documents lie end to end in the sequences of 1024 tokens, so the first token of a sequence has 0 and every other token has 0 or one more than the token before it.
All inputs are finite; a program needn't handle non-finite values.
Results may differ from a plain program's by a relative error of at most 0.023.
Values may be sent and summed in bfloat16 or wider, within the bound.
A program may use at most 320 MiB of HBM per device.

v0:
```python
import math
import jax
import jax.numpy as jnp
from jax import lax
from jax.sharding import PartitionSpec as P

HD = 64
ROT = 16
LAYERS = 2
norm_eps = 1e-05
theta_log = math.log(10000.0)
masked_score = -1e30
contract_rows = (((0,), (0,)), ((), ()))
contract_cols = (((1,), (1,)), ((), ()))


def norm_parts(hidden):
    average = jnp.mean(hidden, axis=-1, keepdims=True)
    centred = hidden - average
    variance = jnp.mean(centred * centred, axis=-1, keepdims=True)
    inverse = lax.rsqrt(variance + norm_eps)
    return (centred * inverse, inverse)


def norm_back(grad_normed, scaled, inverse, norm_weight):
    weighted = grad_normed * norm_weight
    first_mean = jnp.mean(weighted, axis=-1, keepdims=True)
    second_mean = jnp.mean(weighted * scaled, axis=-1, keepdims=True)
    grad_input = inverse * (weighted - first_mean - scaled * second_mean)
    return (grad_input, jnp.sum(grad_normed * scaled, axis=0), jnp.sum(grad_normed, axis=0))


def rotary_tables(positions):
    half_rot = ROT // 2
    frequency = jnp.exp(-(jnp.arange(half_rot, dtype=jnp.float32) * 2.0 / ROT) * theta_log)
    angles = positions.astype(jnp.float32)[:, None] * frequency[None, :]
    return (jnp.cos(angles)[:, None, :], jnp.sin(angles)[:, None, :])


def rotate(values, cos_table, sin_table):
    half_rot = ROT // 2
    first_half = values[..., :half_rot]
    second_half = values[..., half_rot:ROT]
    return jnp.concatenate(
        [
            first_half * cos_table - second_half * sin_table,
            second_half * cos_table + first_half * sin_table,
            values[..., ROT:],
        ],
        axis=-1,
    )


def inner_rows(left, right):
    return lax.dot_general(left, right, contract_rows, preferred_element_type=jnp.float32)


def inner_cols(left, right):
    return lax.dot_general(left, right, contract_cols, preferred_element_type=jnp.float32)


def block_scores(queries, key_rows, positions, number, block_rows, score_scale):
    seq_len = key_rows.shape[0]
    row_start = number * block_rows
    query_block = lax.dynamic_slice_in_dim(queries, row_start, block_rows, 0)
    scores = (
        jnp.einsum("qhd,khd->hqk", query_block, key_rows, preferred_element_type=jnp.float32)
        * score_scale
    )
    row_index = row_start + jnp.arange(block_rows, dtype=jnp.int32)
    first_key = row_index - lax.dynamic_slice_in_dim(positions, row_start, block_rows, 0)
    columns = jnp.arange(seq_len, dtype=jnp.int32)
    allowed = (columns[None, :] <= row_index[:, None]) & (columns[None, :] >= first_key[:, None])
    return (query_block, allowed, jnp.where(allowed[None], scores, masked_score))


def attend_forward(queries, key_rows, values, positions, score_scale):
    seq_len = queries.shape[0]
    block_rows = min(512, seq_len)

    def one_block(number):
        query_block, allowed, scores = block_scores(
            queries, key_rows, positions, number, block_rows, score_scale
        )
        row_max = jnp.max(scores, axis=-1, keepdims=True)
        shifted = jnp.exp(scores - row_max)
        row_sum = jnp.sum(shifted, axis=-1, keepdims=True)
        weights_low = (shifted / row_sum).astype(jnp.bfloat16)
        block_out = jnp.einsum(
            "hqk,khd->qhd", weights_low, values, preferred_element_type=jnp.float32
        )
        return (block_out, row_max + jnp.log(row_sum))

    block_outs, logsums = lax.map(one_block, jnp.arange(seq_len // block_rows, dtype=jnp.int32))
    return (block_outs.reshape(seq_len, -1), logsums)


def attend_back(queries, key_rows, values, positions, logsums, grad_attended, score_scale):
    seq_len = queries.shape[0]
    block_rows = min(512, seq_len)

    def one_block(totals, inputs):
        grad_keys, grad_values = totals
        number, logsum = inputs
        query_block, allowed, scores = block_scores(
            queries, key_rows, positions, number, block_rows, score_scale
        )
        softmax_rows = jnp.exp(scores - logsum)
        grad_block = lax.dynamic_slice_in_dim(grad_attended, number * block_rows, block_rows, 0)
        grad_probs = jnp.einsum(
            "qhd,khd->hqk", grad_block, values, preferred_element_type=jnp.float32
        )
        grad_values = grad_values + jnp.einsum(
            "hqk,qhd->khd",
            softmax_rows.astype(jnp.bfloat16),
            grad_block,
            preferred_element_type=jnp.float32,
        )
        row_inner = jnp.sum(softmax_rows * grad_probs, axis=-1, keepdims=True)
        grad_scores = jnp.where(allowed[None], softmax_rows * (grad_probs - row_inner), 0.0).astype(
            jnp.bfloat16
        )
        grad_query = (
            jnp.einsum("hqk,khd->qhd", grad_scores, key_rows, preferred_element_type=jnp.float32)
            * score_scale
        )
        grad_keys = (
            grad_keys
            + jnp.einsum(
                "hqk,qhd->khd", grad_scores, query_block, preferred_element_type=jnp.float32
            )
            * score_scale
        )
        return ((grad_keys, grad_values), grad_query)

    empty_grad = jnp.zeros(key_rows.shape, jnp.float32)
    numbers = jnp.arange(seq_len // block_rows, dtype=jnp.int32)
    (grad_keys, grad_values), grad_queries = lax.scan(
        one_block, (empty_grad, empty_grad), (numbers, logsums)
    )
    return (grad_queries.reshape(queries.shape), grad_keys, grad_values)


def per_device(
    tokens, positions, norm_gain, norm_bias, w_qkv, b_qkv, w_out, w_gate_up, w_down, cotangent
):
    tensor_rank = lax.axis_index("tensor")
    width_local = w_qkv.shape[3]
    heads_local = width_local // HD
    ff_local = w_gate_up.shape[3]
    local_rows = tokens.shape[0]
    seq_len = positions.shape[0]
    score_scale = 1.0 / math.sqrt(HD)
    cos_table, sin_table = rotary_tables(positions)
    hidden = tokens.astype(jnp.float32)
    kept_state = []
    for layer_index in range(LAYERS):
        gathered = (
            lax.all_gather(w_qkv[layer_index], "dp", axis=0, tiled=True),
            lax.all_gather(w_out[layer_index], "dp", axis=1, tiled=True),
            lax.all_gather(w_gate_up[layer_index], "dp", axis=0, tiled=True),
            lax.all_gather(w_down[layer_index], "dp", axis=1, tiled=True),
        )
        full_qkv, full_out, full_gu, full_down = gathered
        scaled_a, inverse_a = norm_parts(hidden)
        normed_a = (scaled_a * norm_gain[layer_index, 0] + norm_bias[layer_index, 0]).astype(
            jnp.bfloat16
        )
        rows_a = lax.all_gather(normed_a, "tensor", axis=0, tiled=True)
        bias_local = lax.dynamic_slice_in_dim(
            b_qkv[layer_index], tensor_rank * width_local, width_local, 1
        )
        mixed = jnp.dot(
            rows_a,
            full_qkv.reshape(full_qkv.shape[0], 3 * width_local),
            preferred_element_type=jnp.float32,
        ) + bias_local.reshape(3 * width_local)
        mixed = mixed.reshape(seq_len, 3, heads_local, HD)
        queries = rotate(mixed[:, 0], cos_table, sin_table).astype(jnp.bfloat16)
        key_rows = rotate(mixed[:, 1], cos_table, sin_table).astype(jnp.bfloat16)
        values = mixed[:, 2].astype(jnp.bfloat16)
        attended, logsums = attend_forward(queries, key_rows, values, positions, score_scale)
        attended = attended.astype(jnp.bfloat16)

        def project_attn(row_start, row_count, source=attended, weight=full_out):
            return jnp.dot(source, weight, preferred_element_type=jnp.float32)

        branch_a = lax.psum_scatter(
            project_attn(jnp.int32(0), local_rows * lax.axis_size("tensor")).astype(jnp.bfloat16),
            "tensor",
            scatter_dimension=0,
            tiled=True,
        ).astype(jnp.float32)
        hidden_mid = hidden + branch_a
        scaled_b, inverse_b = norm_parts(hidden_mid)
        normed_b = (scaled_b * norm_gain[layer_index, 1] + norm_bias[layer_index, 1]).astype(
            jnp.bfloat16
        )
        rows_b = lax.all_gather(normed_b, "tensor", axis=0, tiled=True)
        gate_up = jnp.dot(
            rows_b,
            full_gu.reshape(full_gu.shape[0], 2 * ff_local),
            preferred_element_type=jnp.float32,
        ).reshape(seq_len, 2, ff_local)
        activated = (jax.nn.silu(gate_up[:, 0]) * gate_up[:, 1]).astype(jnp.bfloat16)

        def project_mlp(row_start, row_count, source=activated, weight=full_down):
            return jnp.dot(source, weight, preferred_element_type=jnp.float32)

        hidden = hidden_mid + lax.psum_scatter(
            project_mlp(jnp.int32(0), local_rows * lax.axis_size("tensor")).astype(jnp.bfloat16),
            "tensor",
            scatter_dimension=0,
            tiled=True,
        ).astype(jnp.float32)
        kept_state.append(
            (
                gathered,
                scaled_a,
                inverse_a,
                rows_a,
                queries,
                key_rows,
                values,
                logsums,
                attended,
                scaled_b,
                inverse_b,
                rows_b,
                gate_up,
                activated,
            )
        )
    activations = hidden.astype(jnp.bfloat16)
    grad = cotangent.astype(jnp.float32)
    weight_parts = [None] * LAYERS
    gain_rows = [None] * LAYERS
    shift_rows = [None] * LAYERS
    qkv_shift_rows = [None] * LAYERS
    for layer_index in reversed(range(LAYERS)):
        (
            gathered,
            scaled_a,
            inverse_a,
            rows_a,
            queries,
            key_rows,
            values,
            logsums,
            attended,
            scaled_b,
            inverse_b,
            rows_b,
            gate_up,
            activated,
        ) = kept_state[layer_index]
        full_qkv, full_out, full_gu, full_down = (
            lax.all_gather(w_qkv[layer_index], "dp", axis=0, tiled=True),
            lax.all_gather(w_out[layer_index], "dp", axis=1, tiled=True),
            lax.all_gather(w_gate_up[layer_index], "dp", axis=0, tiled=True),
            lax.all_gather(w_down[layer_index], "dp", axis=1, tiled=True),
        )
        grad_rows_b = lax.all_gather(grad.astype(jnp.bfloat16), "tensor", axis=0, tiled=True)
        grad_down_weight = inner_rows(activated, grad_rows_b)
        grad_act = inner_cols(grad_rows_b, full_down)
        gate_part = gate_up[:, 0]
        up_part = gate_up[:, 1]
        sigmoid_gate = jax.nn.sigmoid(gate_part)
        grad_gate = grad_act * up_part * sigmoid_gate * (1.0 + gate_part * (1.0 - sigmoid_gate))
        grad_up = grad_act * jax.nn.silu(gate_part)
        grad_gate_up = (
            jnp.stack([grad_gate, grad_up], axis=1)
            .astype(jnp.bfloat16)
            .reshape(seq_len, 2 * ff_local)
        )
        grad_gu_weight = inner_rows(rows_b, grad_gate_up).reshape(full_gu.shape)
        flat_gu = full_gu.reshape(full_gu.shape[0], 2 * ff_local)

        def back_mlp(row_start, row_count, source=grad_gate_up, weight=flat_gu):
            return inner_cols(source, weight)

        grad_normed_b = lax.psum_scatter(
            back_mlp(jnp.int32(0), local_rows * lax.axis_size("tensor")).astype(jnp.bfloat16),
            "tensor",
            scatter_dimension=0,
            tiled=True,
        ).astype(jnp.float32)
        grad_in_b, gain_b, shift_b = norm_back(
            grad_normed_b, scaled_b, inverse_b, norm_gain[layer_index, 1]
        )
        grad = grad + grad_in_b
        grad_rows_a = lax.all_gather(grad.astype(jnp.bfloat16), "tensor", axis=0, tiled=True)
        grad_out_weight = inner_rows(attended, grad_rows_a)
        grad_attended = inner_cols(grad_rows_a, full_out).astype(jnp.bfloat16)
        grad_attended = grad_attended.reshape(seq_len, heads_local, HD)
        grad_queries, grad_keys, grad_values = attend_back(
            queries, key_rows, values, positions, logsums, grad_attended, score_scale
        )
        grad_queries = rotate(grad_queries, cos_table, -sin_table)
        grad_keys = rotate(grad_keys, cos_table, -sin_table)
        grad_mixed = jnp.stack([grad_queries, grad_keys, grad_values], axis=1)
        grad_mixed = grad_mixed.reshape(seq_len, 3 * width_local).astype(jnp.bfloat16)
        qkv_shift_local = jnp.sum(grad_mixed, axis=0, dtype=jnp.float32).reshape(3, width_local)
        qkv_shift_rows[layer_index] = lax.dynamic_update_slice(
            jnp.zeros((3, b_qkv.shape[2]), jnp.float32),
            qkv_shift_local,
            (jnp.int32(0), tensor_rank * width_local),
        )
        grad_qkv_weight = inner_rows(rows_a, grad_mixed).reshape(full_qkv.shape)
        flat_qkv = full_qkv.reshape(full_qkv.shape[0], 3 * width_local)

        def back_attn(row_start, row_count, source=grad_mixed, weight=flat_qkv):
            return inner_cols(source, weight)

        grad_normed_a = lax.psum_scatter(
            back_attn(jnp.int32(0), local_rows * lax.axis_size("tensor")).astype(jnp.bfloat16),
            "tensor",
            scatter_dimension=0,
            tiled=True,
        ).astype(jnp.float32)
        grad_in_a, gain_a, shift_a = norm_back(
            grad_normed_a, scaled_a, inverse_a, norm_gain[layer_index, 0]
        )
        grad = grad + grad_in_a
        gain_rows[layer_index] = jnp.stack([gain_a, gain_b])
        shift_rows[layer_index] = jnp.stack([shift_a, shift_b])
        weight_parts[layer_index] = (
            lax.psum_scatter(
                grad_qkv_weight.astype(jnp.bfloat16), "dp", scatter_dimension=0, tiled=True
            ).astype(jnp.float32),
            lax.psum_scatter(
                grad_out_weight.astype(jnp.bfloat16), "dp", scatter_dimension=1, tiled=True
            ).astype(jnp.float32),
            lax.psum_scatter(
                grad_gu_weight.astype(jnp.bfloat16), "dp", scatter_dimension=0, tiled=True
            ).astype(jnp.float32),
            lax.psum_scatter(
                grad_down_weight.astype(jnp.bfloat16), "dp", scatter_dimension=1, tiled=True
            ).astype(jnp.float32),
        )
    stack_qkv = jnp.stack([weight_parts[number][0] for number in range(LAYERS)])
    stack_out = jnp.stack([weight_parts[number][1] for number in range(LAYERS)])
    stack_gu = jnp.stack([weight_parts[number][2] for number in range(LAYERS)])
    stack_down = jnp.stack([weight_parts[number][3] for number in range(LAYERS)])
    gain_grad, norm_bias_grad, qkv_bias_grad = lax.psum(
        (jnp.stack(gain_rows), jnp.stack(shift_rows), jnp.stack(qkv_shift_rows)), ("dp", "tensor")
    )
    return (
        activations,
        grad,
        gain_grad,
        norm_bias_grad,
        stack_qkv,
        qkv_bias_grad,
        stack_out,
        stack_gu,
        stack_down,
    )


def solution(mesh):
    in_specs = (
        P(("dp", "tensor"), None),
        P("dp"),
        P(),
        P(),
        P(None, "dp", None, "tensor"),
        P(),
        P(None, "tensor", "dp"),
        P(None, "dp", None, "tensor"),
        P(None, "tensor", "dp"),
        P(("dp", "tensor"), None),
    )
    out_specs = (
        P(("dp", "tensor"), None),
        P(("dp", "tensor"), None),
        P(),
        P(),
        P(None, "dp", None, "tensor"),
        P(),
        P(None, "tensor", "dp"),
        P(None, "dp", None, "tensor"),
        P(None, "tensor", "dp"),
    )
    return jax.shard_map(
        per_device, mesh=mesh, in_specs=in_specs, out_specs=out_specs, check_vma=False
    )
```

profile of v0, /device:TPU:1, one launch (start us, length us, event | category | flops | bytes accessed | tf_op | source)
XLA Modules:
  0.0 2722.3 jit_solution(6625782385930977792)
XLA Ops:
  20.9 78.1 %all-gather.25.cloned.1.call-done = bf16[1024,2048]{1,0:T(8,128)(2,1)} async-done(((bf16[256,2048]{1,0:T(8,128)(2,1)}), bf16[1024,2048]{1,0:T(8,128)(2,1)}) %all-gather.25.cloned.1.call-update) | async-done | bytes 4194320 | tf_op jit(solution)/shard_map/all_gather | solution.py:169
  99.0 48.1 %all-gather.41.cloned.1.call-done = bf16[1,2048,3,512]{1,3,2,0:T(8,128)(2,1)} async-done(((bf16[1,256,3,512]{1,3,2,0:T(8,128)(2,1)}), bf16[1,2048,3,512]{1,3,2,0:T(8,128)(2,1)}) %all-gather.41.cloned.1.call-update) | async-done | bytes 6291472 | tf_op jit(solution)/shard_map/all_gather | solution.py:159
  171.9 31.3 %while.54 = (s32[]{:T(128)}, bf16[2,512,8,64]{1,3,2,0:T(8,128)(2,1)}, f32[2,8,512,1]{2,1,3,0:T(8,128)S(1)}, s32[2]{0:T(128)S(1)}, s32[1024]{0:T(1024)S(1)}, /*in...) while((s32[]{:T(128)}, ...), condition=%wide.region_5.6_spmd, body=%wide.region_2.5_spmd.sunk | while | flops 1125643264 | bytes 64628996 | solution.py:94
  219.9 70.5 %reduce-scatter.17.cloned.1.call-done = bf16[256,2048]{1,0:T(8,128)(2,1)} async-done(((bf16[1024,2048]{1,0:T(8,128)(2,1)}), bf16[256,2048]{1,0:T(8,128)(2,1)}) %reduce-scatter.17.cloned.1.call-update) | async-done | bytes 1048592 | tf_op jit(solution)/shard_map/reduce_scatter | solution.py:188
  298.2 63.4 %all-gather.45.cloned.1.call-done = bf16[1,2048,2,1408]{3,1,2,0:T(8,128)(2,1)} async-done(((bf16[1,256,2,1408]{3,1,2,0:T(8,128)(2,1)}), bf16[1,2048,2,1408]{3,1,2,0:T(8,128)(2,1)}) %all-gather.45.cloned.1.call-update) | async-done | bytes 11534352 | tf_op jit(solution)/shard_map/all_gather | solution.py:161
  377.3 66.7 %all-gather.27.cloned.1.call-done = bf16[1024,2048]{1,0:T(8,128)(2,1)} async-done(((bf16[256,2048]{1,0:T(8,128)(2,1)}), bf16[1024,2048]{1,0:T(8,128)(2,1)}) %all-gather.27.cloned.1.call-update) | async-done | bytes 4194320 | tf_op jit(solution)/shard_map/all_gather | solution.py:199
  444.0 17.3 fusion.96
  468.2 21.7 all-gather.47.cloned.1.call-done
  503.3 74.1 %reduce-scatter.19.cloned.1.call-done = bf16[256,2048]{1,0:T(8,128)(2,1)} async-done(((bf16[1024,2048]{1,0:T(8,128)(2,1)}), bf16[256,2048]{1,0:T(8,128)(2,1)}) %reduce-scatter.19.cloned.1.call-update) | async-done | bytes 1048592 | tf_op jit(solution)/shard_map/reduce_scatter | solution.py:210
  583.4 43.5 %all-gather.49.cloned.1.call-done = bf16[1,2048,3,512]{1,3,2,0:T(8,128)(2,1)} async-done(((bf16[1,256,3,512]{1,3,2,0:T(8,128)(2,1)}), bf16[1,2048,3,512]{1,3,2,0:T(8,128)(2,1)}) %all-gather.49.cloned.1.call-update) | async-done | bytes 6291472 | tf_op jit(solution)/shard_map/all_gather | solution.py:159
  626.9 82.4 %all-gather.29.cloned.1.call-done = bf16[1024,2048]{1,0:T(8,128)(2,1)} async-done(((bf16[256,2048]{1,0:T(8,128)(2,1)}), bf16[1024,2048]{1,0:T(8,128)(2,1)}) %all-gather.29.cloned.1.call-update) | async-done | bytes 4194320 | tf_op jit(solution)/shard_map/all_gather | solution.py:169
  735.0 33.6 %while.55 = (s32[]{:T(128)}, bf16[2,512,8,64]{1,3,2,0:T(8,128)(2,1)S(1)}, f32[2,8,512,1]{2,1,3,0:T(8,128)S(1)}, s32[2]{0:T(128)S(1)}, s32[1024]{0:T(1024)S(1)}, ...) while((s32[]{:T(128)}, ...), condition=%wide.region_15.16_spmd, body=%wide.region_12.15_spmd.sunk | while | flops 1125643264 | bytes 56240328 | solution.py:94
  779.1 72.6 %reduce-scatter.21.cloned.1.call-done = bf16[256,2048]{1,0:T(8,128)(2,1)} async-done(((bf16[1024,2048]{1,0:T(8,128)(2,1)}), bf16[256,2048]{1,0:T(8,128)(2,1)}) %reduce-scatter.21.cloned.1.call-update) | async-done | bytes 1048592 | tf_op jit(solution)/shard_map/reduce_scatter | solution.py:188
  857.2 65.2 %all-gather.53.cloned.1.call-done = bf16[1,2048,2,1408]{3,1,2,0:T(8,128)(2,1)} async-done(((bf16[1,256,2,1408]{3,1,2,0:T(8,128)(2,1)}), bf16[1,2048,2,1408]{3,1,2,0:T(8,128)(2,1)}) %all-gather.53.cloned.1.call-update) | async-done | bytes 11534352 | tf_op jit(solution)/shard_map/all_gather | solution.py:161
  938.0 66.9 %all-gather.31.cloned.1.call-done = bf16[1024,2048]{1,0:T(8,128)(2,1)} async-done(((bf16[256,2048]{1,0:T(8,128)(2,1)}), bf16[1024,2048]{1,0:T(8,128)(2,1)}) %all-gather.31.cloned.1.call-update) | async-done | bytes 4194320 | tf_op jit(solution)/shard_map/all_gather | solution.py:199
  1004.8 18.8 fusion.94
  1023.7 62.0 %all-gather.33.cloned.1.call-done = bf16[1024,2048]{1,0:T(8,128)(2,1)} async-done(((bf16[256,2048]{1,0:T(8,128)(2,1)}), bf16[1024,2048]{1,0:T(8,128)(2,1)}) %all-gather.33.cloned.1.call-update) | async-done | bytes 4194320 | tf_op jit(solution)/shard_map/all_gather | solution.py:263
  1085.7 45.2 %all-gather.55.cloned.1.call-done = bf16[1,1408,2048]{2,1,0:T(8,128)(2,1)} async-done(((bf16[1,1408,256]{2,1,0:T(8,128)(2,1)}), bf16[1,1408,2048]{2,1,0:T(8,128)(2,1)}) %all-gather.55.cloned.1.call-update) | async-done | bytes 5767184 | tf_op jit(solution)/shard_map/all_gather | solution.py:162
  1147.5 16.3 bitcast_convert_fusion.1
  1182.0 58.3 %reduce-scatter.25.cloned.1.call-done = bf16[256,2048]{1,0:T(8,128)(2,1)} async-done(((bf16[1024,2048]{1,0:T(8,128)(2,1)}), bf16[256,2048]{1,0:T(8,128)(2,1)}) %reduce-scatter.25.cloned.1.call-update) | async-done | bytes 1048592 | tf_op jit(solution)/shard_map/reduce_scatter | solution.py:282
  1243.1 76.6 %reduce-scatter.23.cloned.1.call-done = bf16[256,2048]{1,0:T(8,128)(2,1)} async-done(((bf16[1024,2048]{1,0:T(8,128)(2,1)}), bf16[256,2048]{1,0:T(8,128)(2,1)}) %reduce-scatter.23.cloned.1.call-update) | async-done | bytes 1048592 | tf_op jit(solution)/shard_map/reduce_scatter | solution.py:210
  1324.5 81.3 %all-gather.35.cloned.1.call-done = bf16[1024,2048]{1,0:T(8,128)(2,1)} async-done(((bf16[256,2048]{1,0:T(8,128)(2,1)}), bf16[1024,2048]{1,0:T(8,128)(2,1)}) %all-gather.35.cloned.1.call-update) | async-done | bytes 4194320 | tf_op jit(solution)/shard_map/all_gather | solution.py:292
  1414.1 183.7 %while.56 = (s32[]{:T(128)}, f32[1024,8,64]{0,2,1:T(8,128)}, f32[1024,8,64]{0,2,1:T(8,128)S(1)}, f32[2,512,8,64]{1,0,3,2:T(2,128)}, s32[2]{0:T(128)S(1)}, /*inde...) while((s32[]{:T(128)}, f32[1024,8,64]{0,2,1:T(8,128)}, ...), condition=%wide.region_25.26_spmd.clone, body=%wide.region_23.25_spmd.clone.sunk | while | flops 2747542528 | bytes 239134992 | solution.py:138
  1437.5 22.9 fusion.302
  1460.4 23.3 bitcast_add_fusion.8
  1486.1 19.6 dynamic_update_slice.48
  1528.8 22.9 fusion.302
  1551.8 23.9 bitcast_add_fusion.8
  1578.0 19.6 dynamic_update_slice.48
  1618.3 75.4 %reduce-scatter.27.cloned.1.call-done = bf16[256,2048]{1,0:T(8,128)(2,1)} async-done(((bf16[1024,2048]{1,0:T(8,128)(2,1)}), bf16[256,2048]{1,0:T(8,128)(2,1)}) %reduce-scatter.27.cloned.1.call-update) | async-done | bytes 1048592 | tf_op jit(solution)/shard_map/reduce_scatter | solution.py:315
  1699.3 81.4 %all-gather.37.cloned.1.call-done = bf16[1024,2048]{1,0:T(8,128)(2,1)} async-done(((bf16[256,2048]{1,0:T(8,128)(2,1)}), bf16[1024,2048]{1,0:T(8,128)(2,1)}) %all-gather.37.cloned.1.call-update) | async-done | bytes 4194320 | tf_op jit(solution)/shard_map/all_gather | solution.py:263
  1814.0 75.4 %reduce-scatter.29.cloned.1.call-done = bf16[256,2048]{1,0:T(8,128)(2,1)} async-done(((bf16[1024,2048]{1,0:T(8,128)(2,1)}), bf16[256,2048]{1,0:T(8,128)(2,1)}) %reduce-scatter.29.cloned.1.call-update) | async-done | bytes 1048592 | tf_op jit(solution)/shard_map/reduce_scatter | solution.py:282
  1933.9 19.1 convolution_convert_fusion
  1968.5 19.2 convolution_convert_fusion.1
  2010.9 198.1 %while.57 = (s32[]{:T(128)}, f32[1024,8,64]{0,2,1:T(8,128)}, f32[1024,8,64]{0,2,1:T(8,128)}, f32[2,512,8,64]{1,0,3,2:T(2,128)}, s32[2]{0:T(128)S(1)}, /*index=5*...) while((s32[]{:T(128)}, f32[1024,8,64]{0,2,1:T(8,128)}, ...), condition=%wide.region_34.35_spmd.clone, body=%wide.region_32.34_spmd.clone.sunk | while | flops 2747542528 | bytes 239134992 | solution.py:138
  2034.5 27.4 %fusion.315 = f32[1,512,8,64]{1,3,2,0:T(8,128)} fusion(bf16[1024,8,64]{0,2,1:T(8,128)(2,1)S(1)} %get-tuple-element.900, f32[8,512,1024]{2,1,0:T(8,128)} %copy-done.1, f32[8,512,1024]{2,1,0:T(8,128)} %fusion.314, pred[512,1024]{1,0:T(8,128)(4,1)S(1)} %fusion.313), kind=kOutput, calls=%fused_computation.87.clone.1 | convolution fusion | flops 558109696 | bytes 36175872 | tf_op jit(solution)/shard_map/while/body/eval_jaxpr/hqk,khd->qhd/dot_general | solution.py:124
  2061.9 24.7 bitcast_add_fusion.10
  2088.9 19.5 dynamic_update_slice.49
  2135.0 26.6 fusion.315
  2161.6 25.4 bitcast_add_fusion.10
  2189.3 19.7 dynamic_update_slice.49
  2259.2 22.5 reduce-scatter.41.cloned.1.call-done
  2290.9 35.7 %reduce-scatter.39.cloned.1.call-done = bf16[512,256]{1,0:T(8,128)(2,1)} async-done(((bf16[512,2048]{1,0:T(8,128)(2,1)}), bf16[512,256]{1,0:T(8,128)(2,1)}) %reduce-scatter.39.cloned.1.call-update) | async-done | bytes 262160 | tf_op jit(solution)/shard_map/reduce_scatter | solution.py:331
  2326.6 44.5 %reduce-scatter.37.cloned.1.call-done = bf16[512,256]{1,0:T(8,128)(2,1)} async-done(((bf16[512,2048]{1,0:T(8,128)(2,1)}), bf16[512,256]{1,0:T(8,128)(2,1)}) %reduce-scatter.37.cloned.1.call-update) | async-done | bytes 262160 | tf_op jit(solution)/shard_map/reduce_scatter | solution.py:331
  2373.2 77.0 %reduce-scatter.31.cloned.1.call-done = bf16[256,2048]{1,0:T(8,128)(2,1)} async-done(((bf16[1024,2048]{1,0:T(8,128)(2,1)}), bf16[256,2048]{1,0:T(8,128)(2,1)}) %reduce-scatter.31.cloned.1.call-update) | async-done | bytes 1048592 | tf_op jit(solution)/shard_map/reduce_scatter | solution.py:315
  2457.2 58.6 %reduce-scatter.35.cloned.1.call-done = bf16[256,3,512]{2,0,1:T(8,128)(2,1)} async-done(((bf16[2048,3,512]{2,0,1:T(8,128)(2,1)}), bf16[256,3,512]{2,0,1:T(8,128)(2,1)}) %reduce-scatter.35.cloned.1.call-update) | async-done | bytes 786448 | tf_op jit(solution)/shard_map/reduce_scatter | solution.py:328
  2515.8 65.6 %reduce-scatter.33.cloned.1.call-done = bf16[256,3,512]{2,0,1:T(8,128)(2,1)} async-done(((bf16[2048,3,512]{2,0,1:T(8,128)(2,1)}), bf16[256,3,512]{2,0,1:T(8,128)(2,1)}) %reduce-scatter.33.cloned.1.call-update) | async-done | bytes 786448 | tf_op jit(solution)/shard_map/reduce_scatter | solution.py:328
  2584.6 126.3 %all-reduce.3.cloned.1.call-done = (f32[2,2,2048]{2,1,0:T(2,128)}, f32[2,2,2048]{2,1,0:T(2,128)}, f32[2,3,2048]{2,0,1:T(2,128)}) async-done(((f32[2,2,2048]{2,1,0:T(2,128)}, f32[2,2,2048]{2,1,0:T(2,128)}, f32[2,3,2048]{2,0,1:T(2,128)}), (f32[2,2,2048]{2,1,0:T(2,128)}, f32[2,2,2048]{2,1,0:T(2,128)}, f32[2,3,2048]{2,0,1:T(2,128)})) %all-reduce.3.cloned.1.call-update) | async-done | bytes 114704 | tf_op jit(solution)/shard_map/psum | solution.py:345
  (483 shorter events, 594.5 us)
Async XLA Ops:
  7.2 91.8 %all-gather.25.cloned.1.call-start = ((), (), s32[]{:S(2)}) async-start(), calls=%async_computation.16 | async-start | bytes 5242880 | tf_op jit(solution)/shard_map/all_gather | solution.py:169
  16.0 131.1 %all-gather.41.cloned.1.call-start = ((), (), s32[]{:S(2)}) async-start(), calls=%async_computation.40 | async-start | bytes 7077888 | tf_op jit(solution)/shard_map/all_gather | solution.py:159
  18.4 189.1 %all-gather.43.cloned.1.call-start = ((), (), s32[]{:S(2)}) async-start(), calls=%async_computation.41 | async-start | bytes 2359296 | tf_op jit(solution)/shard_map/all_gather | solution.py:160
  19.3 271.1 %reduce-scatter.17.cloned.1.call-start = ((), (), s32[]{:S(2)}) async-start(), calls=%async_computation.17 | async-start | bytes 5242880 | tf_op jit(solution)/shard_map/reduce_scatter | solution.py:188
  20.9 149.5 %copy-start.47 = (f32[1024,8]{0,1:T(8,128)}, f32[1024,8]{0,1:T(8,128)S(1)}, u32[]{:S(2)}) copy-start(f32[1024,8]{0,1:T(8,128)S(1)} %get-tuple-element.487) | copy-start | bytes 98308
  20.9 149.5 %copy-start.61 = (f32[1024,8]{0,1:T(8,128)}, f32[1024,8]{0,1:T(8,128)S(1)}, u32[]{:S(2)}) copy-start(f32[1024,8]{0,1:T(8,128)S(1)} %get-tuple-element.486) | copy-start | bytes 98308
  213.9 147.6 %all-gather.45.cloned.1.call-start = ((), (), s32[]{:S(2)}) async-start(), calls=%async_computation.42 | async-start | bytes 12976128 | tf_op jit(solution)/shard_map/all_gather | solution.py:161
  219.9 224.1 %all-gather.27.cloned.1.call-start = ((), (), s32[]{:S(2)}) async-start(), calls=%async_computation.18 | async-start | bytes 5242880 | tf_op jit(solution)/shard_map/all_gather | solution.py:199
  296.8 193.1 %all-gather.47.cloned.1.call-start = ((), (), s32[]{:S(2)}) async-start(), calls=%async_computation.43 | async-start | bytes 6488064 | tf_op jit(solution)/shard_map/all_gather | solution.py:162
  298.1 279.3 %reduce-scatter.19.cloned.1.call-start = ((), (), s32[]{:S(2)}) async-start(), calls=%async_computation.19 | async-start | bytes 5242880 | tf_op jit(solution)/shard_map/reduce_scatter | solution.py:210
  500.8 126.0 %all-gather.49.cloned.1.call-start = ((), (), s32[]{:S(2)}) async-start(), calls=%async_computation.44 | async-start | bytes 7077888 | tf_op jit(solution)/shard_map/all_gather | solution.py:159
  503.2 77.2 %copy-start.67 = (f32[1,1,2048]{2,1,0:T(1,128)S(1)}, f32[1,1,2048]{2,1,0:T(1,128)}, u32[]{:S(2)}) copy-start(f32[1,1,2048]{2,1,0:T(1,128)} %get-tuple-element.480) | copy-start | bytes 24580
  503.2 77.2 %copy-start.79 = (f32[1,1,2048]{2,1,0:T(1,128)S(1)}, f32[1,1,2048]{2,1,0:T(1,128)}, u32[]{:S(2)}) copy-start(f32[1,1,2048]{2,1,0:T(1,128)} %get-tuple-element.484) | copy-start | bytes 24580
  503.2 206.0 %all-gather.29.cloned.1.call-start = ((), (), s32[]{:S(2)}) async-start(), calls=%async_computation.20 | async-start | bytes 5242880 | tf_op jit(solution)/shard_map/all_gather | solution.py:169
  579.5 141.8 %copy-start.88 = (f32[256]{0:T(256)}, f32[256]{0:T(256)S(1)}, u32[]{:S(2)}) copy-start(f32[256]{0:T(256)S(1)} %add_rsqrt_fusion.1) | copy-start | bytes 3076
  581.9 188.2 %all-gather.51.cloned.1.call-start = ((), (), s32[]{:S(2)}) async-start(), calls=%async_computation.45 | async-start | bytes 2359296 | tf_op jit(solution)/shard_map/all_gather | solution.py:160
  582.6 269.1 %reduce-scatter.21.cloned.1.call-start = ((), (), s32[]{:S(2)}) async-start(), calls=%async_computation.21 | async-start | bytes 5242880 | tf_op jit(solution)/shard_map/reduce_scatter | solution.py:188
  776.4 145.9 %all-gather.53.cloned.1.call-start = ((), (), s32[]{:S(2)}) async-start(), calls=%async_computation.46 | async-start | bytes 12976128 | tf_op jit(solution)/shard_map/all_gather | solution.py:161
  779.1 225.8 %all-gather.31.cloned.1.call-start = ((), (), s32[]{:S(2)}) async-start(), calls=%async_computation.22 | async-start | bytes 5242880 | tf_op jit(solution)/shard_map/all_gather | solution.py:199
  856.0 229.7 %all-gather.33.cloned.1.call-start = ((), (), s32[]{:S(2)}) async-start(), calls=%async_computation.24 | async-start | bytes 5242880 | tf_op jit(solution)/shard_map/all_gather | solution.py:263
  856.6 274.3 %all-gather.55.cloned.1.call-start = ((), (), s32[]{:S(2)}) async-start(), calls=%async_computation.47 | async-start | bytes 6488064 | tf_op jit(solution)/shard_map/all_gather | solution.py:162
  857.1 383.2 %reduce-scatter.25.cloned.1.call-start = ((), (), s32[]{:S(2)}) async-start(), calls=%async_computation.25 | async-start | bytes 5242880 | tf_op jit(solution)/shard_map/reduce_scatter | solution.py:282
  1163.8 156.0 %reduce-scatter.23.cloned.1.call-start = ((), (), s32[]{:S(2)}) async-start(), calls=%async_computation.23 | async-start | bytes 5242880 | tf_op jit(solution)/shard_map/reduce_scatter | solution.py:210
  1181.9 137.9 %copy-start.23 = (bf16[256,2048]{1,0:T(8,128)(2,1)S(1)}, bf16[256,2048]{1,0:T(8,128)(2,1)}, u32[]{:S(2)}) copy-start(bf16[256,2048]{1,0:T(8,128)(2,1)} %param.27) | copy-start | bytes 3145732
  1181.9 223.9 %all-gather.35.cloned.1.call-start = ((), (), s32[]{:S(2)}) async-start(), calls=%async_computation.26 | async-start | bytes 5242880 | tf_op jit(solution)/shard_map/all_gather | solution.py:292
  1324.5 369.3 %reduce-scatter.27.cloned.1.call-start = ((), (), s32[]{:S(2)}) async-start(), calls=%async_computation.27 | async-start | bytes 5242880 | tf_op jit(solution)/shard_map/reduce_scatter | solution.py:315
  1324.5 89.6 %copy-start.58 = (f32[2,8,512,1]{2,1,3,0:T(8,128)S(1)}, f32[2,8,512,1]{2,1,3,0:T(8,128)}, u32[]{:S(2)}) copy-start(f32[2,8,512,1]{2,1,3,0:T(8,128)} %copy-done.57) | copy-start | bytes 98308
  1618.3 162.4 %all-gather.37.cloned.1.call-start = ((), (), s32[]{:S(2)}) async-start(), calls=%async_computation.28 | async-start | bytes 5242880 | tf_op jit(solution)/shard_map/all_gather | solution.py:263
  1699.3 190.2 %reduce-scatter.29.cloned.1.call-start = ((), (), s32[]{:S(2)}) async-start(), calls=%async_computation.29 | async-start | bytes 5242880 | tf_op jit(solution)/shard_map/reduce_scatter | solution.py:282
  1813.9 75.5 %copy-start.87 = (f32[256]{0:T(256)S(1)}, f32[256]{0:T(256)}, u32[]{:S(2)}) copy-start(f32[256]{0:T(256)} %copy-done.86) | copy-start | bytes 3076
  1814.0 181.6 %all-gather.39.cloned.1.call-start = ((), (), s32[]{:S(2)}) async-start(), calls=%async_computation.30 | async-start | bytes 5242880 | tf_op jit(solution)/shard_map/all_gather | solution.py:292
  1895.4 359.9 %reduce-scatter.47.cloned.1.call-start = ((), (), s32[]{:S(2)}) async-start(), calls=%async_computation.39 | async-start | bytes 6488064 | tf_op jit(solution)/shard_map/reduce_scatter | solution.py:337
  1906.1 349.2 %reduce-scatter.45.cloned.1.call-start = ((), (), s32[]{:S(2)}) async-start(), calls=%async_computation.38 | async-start | bytes 6488064 | tf_op jit(solution)/shard_map/reduce_scatter | solution.py:337
  1918.7 340.5 %reduce-scatter.43.cloned.1.call-start = ((), (), s32[]{:S(2)}) async-start(), calls=%async_computation.37 | async-start | bytes 12976128 | tf_op jit(solution)/shard_map/reduce_scatter | solution.py:334
  1953.1 328.6 %reduce-scatter.41.cloned.1.call-start = ((), (), s32[]{:S(2)}) async-start(), calls=%async_computation.36 | async-start | bytes 12976128 | tf_op jit(solution)/shard_map/reduce_scatter | solution.py:334
  1987.7 338.8 %reduce-scatter.39.cloned.1.call-start = ((), (), s32[]{:S(2)}) async-start(), calls=%async_computation.35 | async-start | bytes 2359296 | tf_op jit(solution)/shard_map/reduce_scatter | solution.py:331
  1995.5 375.6 %reduce-scatter.37.cloned.1.call-start = ((), (), s32[]{:S(2)}) async-start(), calls=%async_computation.34 | async-start | bytes 2359296 | tf_op jit(solution)/shard_map/reduce_scatter | solution.py:331
  2001.5 448.7 %reduce-scatter.31.cloned.1.call-start = ((), (), s32[]{:S(2)}) async-start(), calls=%async_computation.31 | async-start | bytes 5242880 | tf_op jit(solution)/shard_map/reduce_scatter | solution.py:315
  2228.3 287.6 %reduce-scatter.35.cloned.1.call-start = ((), (), s32[]{:S(2)}) async-start(), calls=%async_computation.33 | async-start | bytes 7077888 | tf_op jit(solution)/shard_map/reduce_scatter | solution.py:328
  2241.3 340.1 %reduce-scatter.33.cloned.1.call-start = ((), (), s32[]{:S(2)}) async-start(), calls=%async_computation.32 | async-start | bytes 7077888 | tf_op jit(solution)/shard_map/reduce_scatter | solution.py:328
  2254.4 456.5 %all-reduce.3.cloned.1.call-start = ((), (), s32[]{:S(2)}) async-start(), calls=%async_computation.48 | async-start | bytes 229376 | tf_op jit(solution)/shard_map/psum | solution.py:345
  2283.9 166.3 %copy-start.4 = (bf16[256,2048]{1,0:T(8,128)(2,1)S(1)}, bf16[256,2048]{1,0:T(8,128)(2,1)}, u32[]{:S(2)}) copy-start(bf16[256,2048]{1,0:T(8,128)(2,1)} %param.18) | copy-start | bytes 3145732
  2283.9 166.3 %copy-start.64 = (f32[1,1,2048]{2,1,0:T(1,128)S(1)}, f32[1,1,2048]{2,1,0:T(1,128)}, u32[]{:S(2)}) copy-start(f32[1,1,2048]{2,1,0:T(1,128)} %copy-done.63) | copy-start | bytes 24580
  2283.9 166.3 %copy-start.85 = (f32[256]{0:T(256)S(1)}, f32[256]{0:T(256)}, u32[]{:S(2)}) copy-start(f32[256]{0:T(256)} %copy-done.84) | copy-start | bytes 3076
  2283.9 166.3 %copy-start.91 = (f32[256]{0:T(256)S(1)}, f32[256]{0:T(256)}, u32[]{:S(2)}) copy-start(f32[256]{0:T(256)} %copy-done.90) | copy-start | bytes 3076
  2290.9 161.6 %copy-start.75 = (f32[2048]{0:T(1024)S(1)}, f32[2048]{0:T(1024)}, u32[]{:S(2)}) copy-start(f32[2048]{0:T(1024)} %get-tuple-element.313) | copy-start | bytes 24580
  2290.9 161.6 %copy-start.74 = (f32[2048]{0:T(1024)S(1)}, f32[2048]{0:T(1024)}, u32[]{:S(2)}) copy-start(f32[2048]{0:T(1024)} %get-tuple-element.326) | copy-start | bytes 24580
  2290.9 163.0 %copy-start.21 = (f32[256,2048]{1,0:T(8,128)S(1)}, f32[256,2048]{1,0:T(8,128)}, u32[]{:S(2)}) copy-start(f32[256,2048]{1,0:T(8,128)} %get-tuple-element.413) | copy-start | bytes 6291460
  (85 other events, 1325.6 us)
Sparse Core Ops, SparseCore 0:
  16.1 82.8 all-gather.24
  101.5 45.5 all-gather.40
  149.6 28.1 all-gather.42
  214.1 76.3 reduce-scatter.16
  292.9 68.5 all-gather.44
  363.6 80.3 all-gather.26
  446.6 43.2 all-gather.46
  501.0 76.3 reduce-scatter.18
  579.2 47.5 all-gather.48
  628.8 80.3 all-gather.28
  711.1 27.1 all-gather.50
  776.5 75.1 reduce-scatter.20
  853.8 68.5 all-gather.52
  924.5 80.3 all-gather.30
  1006.3 79.2 all-gather.32
  1087.5 43.2 all-gather.54
  1163.9 76.3 reduce-scatter.24
  1242.5 77.2 reduce-scatter.22
  1324.6 81.2 all-gather.34
  1618.4 75.2 reduce-scatter.26
  1699.4 81.2 all-gather.36
  1814.1 75.2 reduce-scatter.28
  1895.5 81.2 all-gather.38
  1980.4 57.5 reduce-scatter.46
  2041.5 59.0 reduce-scatter.44
  2104.3 86.8 reduce-scatter.42
  2194.9 86.7 reduce-scatter.40
  2285.3 41.1 reduce-scatter.38
  2329.9 41.1 reduce-scatter.36
  2373.3 76.8 reduce-scatter.30
  2453.6 62.1 reduce-scatter.34
  2519.6 61.7 reduce-scatter.32
  2587.8 123.0 all-reduce.2
where the time goes:
time: 2740 us; the launch traced here: 2720 us
  waiting for transfers between devices  1740 us (64%)
  matrix products  597 us (22%)
  local copies, waits for them, and re-layouts  255 us (9%)
  other arithmetic  105 us (4%)
    all_gather x4, waiting for transfers between devices, per_device(): lax.all_gather(grad.astype(jnp.bfloat16), 'tensor', axis=0, tiled=True)  225 us
    all_gather x2, waiting for transfers between devices, per_device(): rows_a = lax.all_gather(normed_a, 'tensor', axis=0, tiled=True)  160 us
    reduce_scatter x2, waiting for transfers between devices, per_device(): lax.psum_scatter(back_attn(jnp.int32(0), local_rows * lax.axis_size('tens...  152 us
    reduce_scatter x2, waiting for transfers between devices, per_device(): lax.psum_scatter(project_mlp(jnp.int32(0), local_rows * lax.axis_size('te...  151 us
    reduce_scatter x2, waiting for transfers between devices, per_device(): lax.psum_scatter(project_attn(jnp.int32(0), local_rows * lax.axis_size('t...  143 us
    reduce_scatter x2, waiting for transfers between devices, per_device(): lax.psum_scatter(back_mlp(jnp.int32(0), local_rows * lax.axis_size('tenso...  134 us
    all_gather x2, waiting for transfers between devices, per_device(): rows_b = lax.all_gather(normed_b, 'tensor', axis=0, tiled=True)  134 us
    all_gather x2, waiting for transfers between devices, per_device(): lax.all_gather(w_gate_up[layer_index], 'dp', axis=0, tiled=True)  129 us
  transfers between devices with their start and end apart: 33, of which 27 were waited for; matrix products, arithmetic and copies ran while one was open for 22% of the time, Pallas kernels for 0%

commit v1 on v0

--- a/solution.py
+++ b/solution.py
@@ -12,6 +12,17 @@
 masked_score = -1e30
 contract_rows = (((0,), (0,)), ((), ()))
 contract_cols = (((1,), (1,)), ((), ()))
+
+
+def gather_by_hops(x, axis, d):
+    n_dev = lax.axis_size(axis)
+    right = [(i, (i + 1) % n_dev) for i in range(n_dev)]
+    terms = [x]
+    for far in range(1, n_dev):
+        terms = [lax.ppermute(terms[0], axis, right), *terms]
+    full = jnp.concatenate(terms, axis=d)
+    shift = (lax.axis_index(axis) + 1) * terms[-1].shape[d]
+    return jnp.roll(full, shift, axis=d)
 
 
 def norm_parts(hidden):
@@ -196,7 +207,7 @@
         normed_b = (scaled_b * norm_gain[layer_index, 1] + norm_bias[layer_index, 1]).astype(
             jnp.bfloat16
         )
-        rows_b = lax.all_gather(normed_b, "tensor", axis=0, tiled=True)
+        rows_b = gather_by_hops(normed_b, "tensor", 0)
         gate_up = jnp.dot(
             rows_b,
             full_gu.reshape(full_gu.shape[0], 2 * ff_local),

time: 2740 us -> 2590 us (0.945)
  waiting for transfers between devices: 1740 us -> 1550 us
  other arithmetic: 105 us -> 140 us
    all_gather x2 -> x0, waiting for transfers between devices: 134 us -> none  [per_device(): rows_b = lax.all_gather(normed_b, 'tensor', axis=0, tiled=True)]
    ppermute x0 -> x6, waiting for transfers between devices: none -> 99.4 us  [gather_by_hops(): terms = [lax.ppermute(terms[0], axis, right), *terms]]
    all_gather x2, waiting for transfers between devices: 129 us -> 31.5 us  [per_device(): lax.all_gather(w_gate_up[layer_index], 'dp', axis=0, tiled=True)]
    all_gather x4, waiting for transfers between devices: 225 us -> 188 us  [per_device(): lax.all_gather(grad.astype(jnp.bfloat16), 'tensor', axis=0, tiled=True)]
    dynamic_slice x0 -> x2, other arithmetic: none -> 35.6 us  [gather_by_hops(): return jnp.roll(full, shift, axis=d)]
  transfers between devices with their start and end apart: 33 -> 37, of which waited for: 27 -> 28; matrix products, arithmetic and copies ran while one was open for 22% -> 25% of each run, Pallas kernels for 0% -> 0%
where the time goes in v1:
time: 2590 us; the launch traced here: 2570 us
  waiting for transfers between devices  1550 us (60%)
  matrix products  597 us (23%)
  local copies, waits for them, and re-layouts  258 us (10%)
  other arithmetic  140 us (5%)
    all_gather x4, waiting for transfers between devices, per_device(): lax.all_gather(grad.astype(jnp.bfloat16), 'tensor', axis=0, tiled=True)  188 us
    all_gather x2, waiting for transfers between devices, per_device(): rows_a = lax.all_gather(normed_a, 'tensor', axis=0, tiled=True)  161 us
    reduce_scatter x2, waiting for transfers between devices, per_device(): lax.psum_scatter(back_attn(jnp.int32(0), local_rows * lax.axis_size('tens...  153 us
    reduce_scatter x2, waiting for transfers between devices, per_device(): lax.psum_scatter(project_mlp(jnp.int32(0), local_rows * lax.axis_size('te...  151 us
    reduce_scatter x2, waiting for transfers between devices, per_device(): lax.psum_scatter(project_attn(jnp.int32(0), local_rows * lax.axis_size('t...  140 us
    reduce_scatter x2, waiting for transfers between devices, per_device(): lax.psum_scatter(back_mlp(jnp.int32(0), local_rows * lax.axis_size('tenso...  134 us
    psum x1, waiting for transfers between devices, per_device(): lax.psum((jnp.stack(gain_rows), jnp.stack(shift_rows), jnp.stack(qkv_shif...  126 us
    reduce_scatter x2, waiting for transfers between devices, per_device(): lax.psum_scatter(grad_qkv_weight.astype(jnp.bfloat16), 'dp', scatter_dime...  124 us
  transfers between devices with their start and end apart: 37, of which 28 were waited for; matrix products, arithmetic and copies ran while one was open for 25% of the time, Pallas kernels for 0%

profile of v1, /device:TPU:1, one launch (start us, length us, event | category | flops | bytes accessed | tf_op | source)
XLA Modules:
  0.0 2569.5 jit_solution(12648790781538886335)
XLA Ops:
  20.9 78.2 %all-gather.23.cloned.1.call-done = bf16[1024,2048]{1,0:T(8,128)(2,1)} async-done(((bf16[256,2048]{1,0:T(8,128)(2,1)}), bf16[1024,2048]{1,0:T(8,128)(2,1)}) %all-gather.23.cloned.1.call-update) | async-done | bytes 4194320 | tf_op jit(solution)/shard_map/all_gather | solution.py:180
  99.1 48.1 %all-gather.35.cloned.1.call-done = bf16[1,2048,3,512]{1,3,2,0:T(8,128)(2,1)} async-done(((bf16[1,256,3,512]{1,3,2,0:T(8,128)(2,1)}), bf16[1,2048,3,512]{1,3,2,0:T(8,128)(2,1)}) %all-gather.35.cloned.1.call-update) | async-done | bytes 6291472 | tf_op jit(solution)/shard_map/all_gather | solution.py:170
  171.8 31.3 %while.54 = (s32[]{:T(128)}, bf16[2,512,8,64]{1,3,2,0:T(8,128)(2,1)}, f32[2,8,512,1]{2,1,3,0:T(8,128)S(1)}, s32[2]{0:T(128)S(1)}, s32[1024]{0:T(1024)S(1)}, /*in...) while((s32[]{:T(128)}, ...), condition=%wide.region_5.6_spmd, body=%wide.region_2.5_spmd.sunk | while | flops 1125643264 | bytes 64628996 | solution.py:105
  221.8 68.5 %reduce-scatter.17.cloned.1.call-done = bf16[256,2048]{1,0:T(8,128)(2,1)} async-done(((bf16[1024,2048]{1,0:T(8,128)(2,1)}), bf16[256,2048]{1,0:T(8,128)(2,1)}) %reduce-scatter.17.cloned.1.call-update) | async-done | bytes 1048592 | tf_op jit(solution)/shard_map/reduce_scatter | solution.py:199
  295.7 24.7 collective-permute-done
  321.3 25.1 collective-permute-done.1
  390.4 17.6 fusion.96
  428.6 74.2 %reduce-scatter.19.cloned.1.call-done = bf16[256,2048]{1,0:T(8,128)(2,1)} async-done(((bf16[1024,2048]{1,0:T(8,128)(2,1)}), bf16[256,2048]{1,0:T(8,128)(2,1)}) %reduce-scatter.19.cloned.1.call-update) | async-done | bytes 1048592 | tf_op jit(solution)/shard_map/reduce_scatter | solution.py:221
  508.6 43.6 %all-gather.43.cloned.1.call-done = bf16[1,2048,3,512]{1,3,2,0:T(8,128)(2,1)} async-done(((bf16[1,256,3,512]{1,3,2,0:T(8,128)(2,1)}), bf16[1,2048,3,512]{1,3,2,0:T(8,128)(2,1)}) %all-gather.43.cloned.1.call-update) | async-done | bytes 6291472 | tf_op jit(solution)/shard_map/all_gather | solution.py:170
  552.3 82.5 %all-gather.25.cloned.1.call-done = bf16[1024,2048]{1,0:T(8,128)(2,1)} async-done(((bf16[256,2048]{1,0:T(8,128)(2,1)}), bf16[1024,2048]{1,0:T(8,128)(2,1)}) %all-gather.25.cloned.1.call-update) | async-done | bytes 4194320 | tf_op jit(solution)/shard_map/all_gather | solution.py:180
  660.4 33.8 %while.55 = (s32[]{:T(128)}, bf16[2,512,8,64]{1,3,2,0:T(8,128)(2,1)S(1)}, f32[2,8,512,1]{2,1,3,0:T(8,128)S(1)}, s32[2]{0:T(128)S(1)}, s32[1024]{0:T(1024)S(1)}, ...) while((s32[]{:T(128)}, ...), condition=%wide.region_15.17_spmd, body=%wide.region_12.16_spmd.sunk | while | flops 1125643264 | bytes 56240328 | solution.py:105
  706.0 71.3 %reduce-scatter.21.cloned.1.call-done = bf16[256,2048]{1,0:T(8,128)(2,1)} async-done(((bf16[1024,2048]{1,0:T(8,128)(2,1)}), bf16[256,2048]{1,0:T(8,128)(2,1)}) %reduce-scatter.21.cloned.1.call-update) | async-done | bytes 1048592 | tf_op jit(solution)/shard_map/reduce_scatter | solution.py:199
  781.9 24.7 collective-permute-done.3
  806.5 24.9 collective-permute-done.4
  831.5 16.4 all-gather.47.cloned.1.call-done
  863.3 22.1 fusion.122
  887.4 17.5 fusion.94
  904.9 25.0 all-gather.27.cloned.1.call-done
  929.9 45.2 %all-gather.49.cloned.1.call-done = bf16[1,1408,2048]{2,1,0:T(8,128)(2,1)} async-done(((bf16[1,1408,256]{2,1,0:T(8,128)(2,1)}), bf16[1,1408,2048]{2,1,0:T(8,128)(2,1)}) %all-gather.49.cloned.1.call-update) | async-done | bytes 5767184 | tf_op jit(solution)/shard_map/all_gather | solution.py:173
  1026.1 58.7 %reduce-scatter.25.cloned.1.call-done = bf16[256,2048]{1,0:T(8,128)(2,1)} async-done(((bf16[1024,2048]{1,0:T(8,128)(2,1)}), bf16[256,2048]{1,0:T(8,128)(2,1)}) %reduce-scatter.25.cloned.1.call-update) | async-done | bytes 1048592 | tf_op jit(solution)/shard_map/reduce_scatter | solution.py:293
  1087.6 76.7 %reduce-scatter.23.cloned.1.call-done = bf16[256,2048]{1,0:T(8,128)(2,1)} async-done(((bf16[1024,2048]{1,0:T(8,128)(2,1)}), bf16[256,2048]{1,0:T(8,128)(2,1)}) %reduce-scatter.23.cloned.1.call-update) | async-done | bytes 1048592 | tf_op jit(solution)/shard_map/reduce_scatter | solution.py:221
  1169.1 81.3 %all-gather.29.cloned.1.call-done = bf16[1024,2048]{1,0:T(8,128)(2,1)} async-done(((bf16[256,2048]{1,0:T(8,128)(2,1)}), bf16[1024,2048]{1,0:T(8,128)(2,1)}) %all-gather.29.cloned.1.call-update) | async-done | bytes 4194320 | tf_op jit(solution)/shard_map/all_gather | solution.py:303
  1258.6 183.8 %while.56 = (s32[]{:T(128)}, f32[1024,8,64]{0,2,1:T(8,128)}, f32[1024,8,64]{0,2,1:T(8,128)S(1)}, f32[2,512,8,64]{1,0,3,2:T(2,128)}, s32[2]{0:T(128)S(1)}, /*inde...) while((s32[]{:T(128)}, f32[1024,8,64]{0,2,1:T(8,128)}, ...), condition=%wide.region_25.27_spmd.clone, body=%wide.region_23.26_spmd.clone.sunk | while | flops 2747542528 | bytes 239134992 | solution.py:149
  1282.0 22.9 fusion.318
  1305.0 23.3 bitcast_add_fusion.8
  1330.6 19.6 dynamic_update_slice.48
  1373.4 22.9 fusion.318
  1396.4 23.9 bitcast_add_fusion.8
  1422.6 19.6 dynamic_update_slice.48
  1462.9 75.4 %reduce-scatter.27.cloned.1.call-done = bf16[256,2048]{1,0:T(8,128)(2,1)} async-done(((bf16[1024,2048]{1,0:T(8,128)(2,1)}), bf16[256,2048]{1,0:T(8,128)(2,1)}) %reduce-scatter.27.cloned.1.call-update) | async-done | bytes 1048592 | tf_op jit(solution)/shard_map/reduce_scatter | solution.py:326
  1545.2 81.3 %all-gather.31.cloned.1.call-done = bf16[1024,2048]{1,0:T(8,128)(2,1)} async-done(((bf16[256,2048]{1,0:T(8,128)(2,1)}), bf16[1024,2048]{1,0:T(8,128)(2,1)}) %all-gather.31.cloned.1.call-update) | async-done | bytes 4194320 | tf_op jit(solution)/shard_map/all_gather | solution.py:274
  1659.8 75.4 %reduce-scatter.29.cloned.1.call-done = bf16[256,2048]{1,0:T(8,128)(2,1)} async-done(((bf16[1024,2048]{1,0:T(8,128)(2,1)}), bf16[256,2048]{1,0:T(8,128)(2,1)}) %reduce-scatter.29.cloned.1.call-update) | async-done | bytes 1048592 | tf_op jit(solution)/shard_map/reduce_scatter | solution.py:293
  1780.9 19.1 convolution_convert_fusion
  1815.4 19.2 convolution_convert_fusion.1
  1857.9 199.0 %while.57 = (s32[]{:T(128)}, f32[1024,8,64]{0,2,1:T(8,128)}, f32[1024,8,64]{0,2,1:T(8,128)}, f32[2,512,8,64]{1,0,3,2:T(2,128)}, s32[2]{0:T(128)S(1)}, /*index=5*...) while((s32[]{:T(128)}, f32[1024,8,64]{0,2,1:T(8,128)}, ...), condition=%wide.region_34.36_spmd.clone, body=%wide.region_32.35_spmd.clone.sunk | while | flops 2747542528 | bytes 239134992 | solution.py:149
  1881.5 27.7 %fusion.331 = f32[1,512,8,64]{1,3,2,0:T(8,128)} fusion(bf16[1024,8,64]{0,2,1:T(8,128)(2,1)S(1)} %get-tuple-element.901, f32[8,512,1024]{2,1,0:T(8,128)} %copy-done.1, f32[8,512,1024]{2,1,0:T(8,128)} %fusion.330, pred[512,1024]{1,0:T(8,128)(4,1)S(1)} %fusion.329), kind=kOutput, calls=%fused_computation.87.clone.1 | convolution fusion | flops 558109696 | bytes 36175872 | tf_op jit(solution)/shard_map/while/body/eval_jaxpr/hqk,khd->qhd/dot_general | solution.py:135
  1909.3 24.7 bitcast_add_fusion.10
  1936.3 19.5 dynamic_update_slice.49
  1982.3 27.3 %fusion.331 = f32[1,512,8,64]{1,3,2,0:T(8,128)} fusion(bf16[1024,8,64]{0,2,1:T(8,128)(2,1)S(1)} %get-tuple-element.901, f32[8,512,1024]{2,1,0:T(8,128)} %copy-done.1, f32[8,512,1024]{2,1,0:T(8,128)} %fusion.330, pred[512,1024]{1,0:T(8,128)(4,1)S(1)} %fusion.329), kind=kOutput, calls=%fused_computation.87.clone.1 | convolution fusion | flops 558109696 | bytes 36175872 | tf_op jit(solution)/shard_map/while/body/eval_jaxpr/hqk,khd->qhd/dot_general | solution.py:135
  2009.6 25.3 bitcast_add_fusion.10
  2037.2 19.7 dynamic_update_slice.49
  2107.3 21.7 reduce-scatter.41.cloned.1.call-done
  2138.2 35.5 %reduce-scatter.39.cloned.1.call-done = bf16[512,256]{1,0:T(8,128)(2,1)} async-done(((bf16[512,2048]{1,0:T(8,128)(2,1)}), bf16[512,256]{1,0:T(8,128)(2,1)}) %reduce-scatter.39.cloned.1.call-update) | async-done | bytes 262160 | tf_op jit(solution)/shard_map/reduce_scatter | solution.py:342
  2173.7 44.4 %reduce-scatter.37.cloned.1.call-done = bf16[512,256]{1,0:T(8,128)(2,1)} async-done(((bf16[512,2048]{1,0:T(8,128)(2,1)}), bf16[512,256]{1,0:T(8,128)(2,1)}) %reduce-scatter.37.cloned.1.call-update) | async-done | bytes 262160 | tf_op jit(solution)/shard_map/reduce_scatter | solution.py:342
  2220.2 77.1 %reduce-scatter.31.cloned.1.call-done = bf16[256,2048]{1,0:T(8,128)(2,1)} async-done(((bf16[1024,2048]{1,0:T(8,128)(2,1)}), bf16[256,2048]{1,0:T(8,128)(2,1)}) %reduce-scatter.31.cloned.1.call-update) | async-done | bytes 1048592 | tf_op jit(solution)/shard_map/reduce_scatter | solution.py:326
  2304.4 58.6 %reduce-scatter.35.cloned.1.call-done = bf16[256,3,512]{2,0,1:T(8,128)(2,1)} async-done(((bf16[2048,3,512]{2,0,1:T(8,128)(2,1)}), bf16[256,3,512]{2,0,1:T(8,128)(2,1)}) %reduce-scatter.35.cloned.1.call-update) | async-done | bytes 786448 | tf_op jit(solution)/shard_map/reduce_scatter | solution.py:339
  2363.0 65.4 %reduce-scatter.33.cloned.1.call-done = bf16[256,3,512]{2,0,1:T(8,128)(2,1)} async-done(((bf16[2048,3,512]{2,0,1:T(8,128)(2,1)}), bf16[256,3,512]{2,0,1:T(8,128)(2,1)}) %reduce-scatter.33.cloned.1.call-update) | async-done | bytes 786448 | tf_op jit(solution)/shard_map/reduce_scatter | solution.py:339
  2431.6 126.4 %all-reduce.3.cloned.1.call-done = (f32[2,2,2048]{2,1,0:T(2,128)}, f32[2,2,2048]{2,1,0:T(2,128)}, f32[2,3,2048]{2,0,1:T(2,128)}) async-done(((f32[2,2,2048]{2,1,0:T(2,128)}, f32[2,2,2048]{2,1,0:T(2,128)}, f32[2,3,2048]{2,0,1:T(2,128)}), (f32[2,2,2048]{2,1,0:T(2,128)}, f32[2,2,2048]{2,1,0:T(2,128)}, f32[2,3,2048]{2,0,1:T(2,128)})) %all-reduce.3.cloned.1.call-update) | async-done | bytes 114704 | tf_op jit(solution)/shard_map/psum | solution.py:356
  (495 shorter events, 644.3 us)
Async XLA Ops:
  7.2 91.9 %all-gather.23.cloned.1.call-start = ((), (), s32[]{:S(2)}) async-start(), calls=%async_computation.16 | async-start | bytes 5242880 | tf_op jit(solution)/shard_map/all_gather | solution.py:180
  16.1 131.1 %all-gather.35.cloned.1.call-start = ((), (), s32[]{:S(2)}) async-start(), calls=%async_computation.38 | async-start | bytes 7077888 | tf_op jit(solution)/shard_map/all_gather | solution.py:170
  18.4 189.1 %all-gather.37.cloned.1.call-start = ((), (), s32[]{:S(2)}) async-start(), calls=%async_computation.39 | async-start | bytes 2359296 | tf_op jit(solution)/shard_map/all_gather | solution.py:171
  19.3 271.1 %reduce-scatter.17.cloned.1.call-start = ((), (), s32[]{:S(2)}) async-start(), calls=%async_computation.17 | async-start | bytes 5242880 | tf_op jit(solution)/shard_map/reduce_scatter | solution.py:199
  20.9 149.5 %copy-start.48 = (f32[1024,8]{0,1:T(8,128)}, f32[1024,8]{0,1:T(8,128)S(1)}, u32[]{:S(2)}) copy-start(f32[1024,8]{0,1:T(8,128)S(1)} %get-tuple-element.488) | copy-start | bytes 98308
  20.9 149.5 %copy-start.62 = (f32[1024,8]{0,1:T(8,128)}, f32[1024,8]{0,1:T(8,128)S(1)}, u32[]{:S(2)}) copy-start(f32[1024,8]{0,1:T(8,128)S(1)} %get-tuple-element.487) | copy-start | bytes 98308
  213.9 147.6 %all-gather.39.cloned.1.call-start = ((), (), s32[]{:S(2)}) async-start(), calls=%async_computation.40 | async-start | bytes 12976128 | tf_op jit(solution)/shard_map/all_gather | solution.py:172
  219.8 195.5 %all-gather.41.cloned.1.call-start = ((), (), s32[]{:S(2)}) async-start(), calls=%async_computation.41 | async-start | bytes 6488064 | tf_op jit(solution)/shard_map/all_gather | solution.py:173
  221.8 281.0 %reduce-scatter.19.cloned.1.call-start = ((), (), s32[]{:S(2)}) async-start(), calls=%async_computation.18 | async-start | bytes 5242880 | tf_op jit(solution)/shard_map/reduce_scatter | solution.py:221
  294.4 25.9 %collective-permute-start = (bf16[256,2048]{1,0:T(8,128)(2,1)S(1)}, bf16[256,2048]{1,0:T(8,128)(2,1)S(1)}, u32[]{:S(2)}, u32[]{:S(2)}) collective-permute-start(bf16[256,2048]{1,0:T(8,128)(2,1)S(1)} %add_convert_fusion.3), channel_id=1, source_target_pairs={{0,1},{1,2},{2,3},{3,0},{4,5},{5,6},{6,7},{7,4},{8,9},{9,10},{10,1... | collective-permute-start | bytes 3145736 | tf_op jit(solution)/shard_map/ppermute | solution.py:22
  321.3 25.1 collective-permute-start.1
  346.4 30.5 %collective-permute-start.2 = (bf16[256,2048]{1,0:T(8,128)(2,1)}, bf16[256,2048]{1,0:T(8,128)(2,1)}, u32[]{:S(2)}, u32[]{:S(2)}) collective-permute-start(bf16[256,2048]{1,0:T(8,128)(2,1)} %collective-permute-done.1), channel_id=1, source_target_pairs={{0,1},{1,2},{2,3},{3,0},{4,5},{5,6},{6,7},{7,4},{8,9},{9,10},{10,1... | collective-permute-start | bytes 3145736 | tf_op jit(solution)/shard_map/ppermute | solution.py:22
  426.2 126.0 %all-gather.43.cloned.1.call-start = ((), (), s32[]{:S(2)}) async-start(), calls=%async_computation.42 | async-start | bytes 7077888 | tf_op jit(solution)/shard_map/all_gather | solution.py:170
  428.6 206.2 %all-gather.25.cloned.1.call-start = ((), (), s32[]{:S(2)}) async-start(), calls=%async_computation.19 | async-start | bytes 5242880 | tf_op jit(solution)/shard_map/all_gather | solution.py:180
  504.5 142.1 %copy-start.84 = (f32[256]{0:T(256)}, f32[256]{0:T(256)S(1)}, u32[]{:S(2)}) copy-start(f32[256]{0:T(256)S(1)} %broadcast_multiply_fusion.9) | copy-start | bytes 3076
  504.9 141.7 %copy-start.90 = (f32[256]{0:T(256)}, f32[256]{0:T(256)S(1)}, u32[]{:S(2)}) copy-start(f32[256]{0:T(256)S(1)} %add_rsqrt_fusion.1) | copy-start | bytes 3076
  507.3 188.3 %all-gather.45.cloned.1.call-start = ((), (), s32[]{:S(2)}) async-start(), calls=%async_computation.43 | async-start | bytes 2359296 | tf_op jit(solution)/shard_map/all_gather | solution.py:171
  507.9 269.4 %reduce-scatter.21.cloned.1.call-start = ((), (), s32[]{:S(2)}) async-start(), calls=%async_computation.20 | async-start | bytes 5242880 | tf_op jit(solution)/shard_map/reduce_scatter | solution.py:199
  702.0 145.9 %all-gather.47.cloned.1.call-start = ((), (), s32[]{:S(2)}) async-start(), calls=%async_computation.44 | async-start | bytes 12976128 | tf_op jit(solution)/shard_map/all_gather | solution.py:172
  704.6 225.3 %all-gather.27.cloned.1.call-start = ((), (), s32[]{:S(2)}) async-start(), calls=%async_computation.22 | async-start | bytes 5242880 | tf_op jit(solution)/shard_map/all_gather | solution.py:274
  705.4 269.7 %all-gather.49.cloned.1.call-start = ((), (), s32[]{:S(2)}) async-start(), calls=%async_computation.45 | async-start | bytes 6488064 | tf_op jit(solution)/shard_map/all_gather | solution.py:173
  706.0 378.9 %reduce-scatter.25.cloned.1.call-start = ((), (), s32[]{:S(2)}) async-start(), calls=%async_computation.23 | async-start | bytes 5242880 | tf_op jit(solution)/shard_map/reduce_scatter | solution.py:293
  780.6 25.9 %collective-permute-start.3 = (bf16[256,2048]{1,0:T(8,128)(2,1)S(1)}, bf16[256,2048]{1,0:T(8,128)(2,1)S(1)}, u32[]{:S(2)}, u32[]{:S(2)}) collective-permute-start(bf16[256,2048]{1,0:T(8,128)(2,1)S(1)} %add_convert_fusion.1), channel_id=1, source_target_pairs={{0,1},{1,2},{2,3},{3,0},{4,5},{5,6},{6,7},{7,4},{8,9},{9,10},{10,1... | collective-permute-start | bytes 3145736 | tf_op jit(solution)/shard_map/ppermute | solution.py:22
  806.5 25.0 collective-permute-start.4
  831.5 31.8 %collective-permute-start.5 = (bf16[256,2048]{1,0:T(8,128)(2,1)S(1)}, bf16[256,2048]{1,0:T(8,128)(2,1)}, u32[]{:S(2)}, u32[]{:S(2)}) collective-permute-start(bf16[256,2048]{1,0:T(8,128)(2,1)S(1)} %collective-permute-done.4), channel_id=1, source_target_pairs={{0,1},{1,2},{2,3},{3,0},{4,5},{5,6},{6,7},{7,4},{8,9},{9,10},{10,1... | collective-permute-start | bytes 3145736 | tf_op jit(solution)/shard_map/ppermute | solution.py:22
  1008.3 156.0 %reduce-scatter.23.cloned.1.call-start = ((), (), s32[]{:S(2)}) async-start(), calls=%async_computation.21 | async-start | bytes 5242880 | tf_op jit(solution)/shard_map/reduce_scatter | solution.py:221
  1026.1 224.3 %all-gather.29.cloned.1.call-start = ((), (), s32[]{:S(2)}) async-start(), calls=%async_computation.24 | async-start | bytes 5242880 | tf_op jit(solution)/shard_map/all_gather | solution.py:303
  1169.0 369.4 %reduce-scatter.27.cloned.1.call-start = ((), (), s32[]{:S(2)}) async-start(), calls=%async_computation.25 | async-start | bytes 5242880 | tf_op jit(solution)/shard_map/reduce_scatter | solution.py:326
  1462.9 163.6 %all-gather.31.cloned.1.call-start = ((), (), s32[]{:S(2)}) async-start(), calls=%async_computation.26 | async-start | bytes 5242880 | tf_op jit(solution)/shard_map/all_gather | solution.py:274
  1545.1 190.1 %reduce-scatter.29.cloned.1.call-start = ((), (), s32[]{:S(2)}) async-start(), calls=%async_computation.27 | async-start | bytes 5242880 | tf_op jit(solution)/shard_map/reduce_scatter | solution.py:293
  1659.8 182.8 %all-gather.33.cloned.1.call-start = ((), (), s32[]{:S(2)}) async-start(), calls=%async_computation.28 | async-start | bytes 5242880 | tf_op jit(solution)/shard_map/all_gather | solution.py:303
  1742.4 360.9 %reduce-scatter.47.cloned.1.call-start = ((), (), s32[]{:S(2)}) async-start(), calls=%async_computation.37 | async-start | bytes 6488064 | tf_op jit(solution)/shard_map/reduce_scatter | solution.py:348
  1753.1 350.2 %reduce-scatter.45.cloned.1.call-start = ((), (), s32[]{:S(2)}) async-start(), calls=%async_computation.36 | async-start | bytes 6488064 | tf_op jit(solution)/shard_map/reduce_scatter | solution.py:348
  1765.7 341.6 %reduce-scatter.43.cloned.1.call-start = ((), (), s32[]{:S(2)}) async-start(), calls=%async_computation.35 | async-start | bytes 12976128 | tf_op jit(solution)/shard_map/reduce_scatter | solution.py:345
  1800.1 329.0 %reduce-scatter.41.cloned.1.call-start = ((), (), s32[]{:S(2)}) async-start(), calls=%async_computation.34 | async-start | bytes 12976128 | tf_op jit(solution)/shard_map/reduce_scatter | solution.py:345
  1834.7 339.1 %reduce-scatter.39.cloned.1.call-start = ((), (), s32[]{:S(2)}) async-start(), calls=%async_computation.33 | async-start | bytes 2359296 | tf_op jit(solution)/shard_map/reduce_scatter | solution.py:342
  1842.4 375.7 %reduce-scatter.37.cloned.1.call-start = ((), (), s32[]{:S(2)}) async-start(), calls=%async_computation.32 | async-start | bytes 2359296 | tf_op jit(solution)/shard_map/reduce_scatter | solution.py:342
  1848.5 448.8 %reduce-scatter.31.cloned.1.call-start = ((), (), s32[]{:S(2)}) async-start(), calls=%async_computation.29 | async-start | bytes 5242880 | tf_op jit(solution)/shard_map/reduce_scatter | solution.py:326
  2076.1 286.9 %reduce-scatter.35.cloned.1.call-start = ((), (), s32[]{:S(2)}) async-start(), calls=%async_computation.31 | async-start | bytes 7077888 | tf_op jit(solution)/shard_map/reduce_scatter | solution.py:339
  2089.4 339.0 %reduce-scatter.33.cloned.1.call-start = ((), (), s32[]{:S(2)}) async-start(), calls=%async_computation.30 | async-start | bytes 7077888 | tf_op jit(solution)/shard_map/reduce_scatter | solution.py:339
  2102.4 455.6 %all-reduce.3.cloned.1.call-start = ((), (), s32[]{:S(2)}) async-start(), calls=%async_computation.46 | async-start | bytes 229376 | tf_op jit(solution)/shard_map/psum | solution.py:356
  2131.2 166.2 %copy-start.4 = (bf16[256,2048]{1,0:T(8,128)(2,1)S(1)}, bf16[256,2048]{1,0:T(8,128)(2,1)}, u32[]{:S(2)}) copy-start(bf16[256,2048]{1,0:T(8,128)(2,1)} %param.20) | copy-start | bytes 3145732
  2131.2 166.2 %copy-start.65 = (f32[1,1,2048]{2,1,0:T(1,128)S(1)}, f32[1,1,2048]{2,1,0:T(1,128)}, u32[]{:S(2)}) copy-start(f32[1,1,2048]{2,1,0:T(1,128)} %copy-done.64) | copy-start | bytes 24580
  2131.2 166.2 %copy-start.87 = (f32[256]{0:T(256)S(1)}, f32[256]{0:T(256)}, u32[]{:S(2)}) copy-start(f32[256]{0:T(256)} %copy-done.86) | copy-start | bytes 3076
  2131.2 166.1 %copy-start.93 = (f32[256]{0:T(256)S(1)}, f32[256]{0:T(256)}, u32[]{:S(2)}) copy-start(f32[256]{0:T(256)} %copy-done.92) | copy-start | bytes 3076
  2131.2 168.4 %copy-start.76 = (f32[2048]{0:T(1024)S(1)}, f32[2048]{0:T(1024)}, u32[]{:S(2)}) copy-start(f32[2048]{0:T(1024)} %get-tuple-element.314) | copy-start | bytes 24580
  2131.2 168.5 %copy-start.75 = (f32[2048]{0:T(1024)S(1)}, f32[2048]{0:T(1024)}, u32[]{:S(2)}) copy-start(f32[2048]{0:T(1024)} %get-tuple-element.327) | copy-start | bytes 24580
  2138.2 162.8 %copy-start.21 = (f32[256,2048]{1,0:T(8,128)S(1)}, f32[256,2048]{1,0:T(8,128)}, u32[]{:S(2)}) copy-start(f32[256,2048]{1,0:T(8,128)} %get-tuple-element.414) | copy-start | bytes 6291460
  (91 other events, 2033.5 us)
Sparse Core Ops, SparseCore 0:
  16.2 82.8 all-gather.22
  101.5 45.5 all-gather.34
  149.6 28.1 all-gather.36
  214.0 76.3 reduce-scatter.16
  292.9 68.5 all-gather.38
  363.4 44.3 all-gather.40
  426.4 76.3 reduce-scatter.18
  504.7 47.5 all-gather.42
  554.4 80.3 all-gather.24
  636.5 27.1 all-gather.44
  702.1 75.1 reduce-scatter.20
  779.2 68.5 all-gather.46
  849.5 80.3 all-gather.26
  931.8 43.2 all-gather.48
  1008.4 76.3 reduce-scatter.24
  1087.0 77.2 reduce-scatter.22
  1169.1 81.2 all-gather.28
  1463.0 75.3 reduce-scatter.26
  1545.2 81.2 all-gather.30
  1659.9 75.3 reduce-scatter.28
  1742.5 81.2 all-gather.32
  1827.6 57.5 reduce-scatter.46
  1888.6 59.0 reduce-scatter.44
  1951.5 86.7 reduce-scatter.42
  2042.2 86.7 reduce-scatter.40
  2132.5 41.1 reduce-scatter.38
  2176.9 41.2 reduce-scatter.36
  2220.5 76.7 reduce-scatter.30
  2300.7 62.2 reduce-scatter.34
  2366.6 61.7 reduce-scatter.32
  2434.9 123.0 all-reduce.2
